TPU v7x, 256 devices: a whole 4x4x8 slice. The times are simulated.
256 devices in a mesh: section: 2 (over x_lo), blk: 128 (over x_hi, y, z, core).
Axes of the slice: x: 4 (x_hi: 2, x_lo: 2; x = x_hi * 2 + x_lo), y: 4, z: 8, core: 2. Of those that a mesh axis runs over, the one named last changes fastest.
Arguments:
- raw_traces: bfloat16 [1024, 8192], P('blk', 'section'), may hold values from -6 to 6
- valid_mask: int32 [1024, 8], P('blk', 'section'), may hold values from 0 to 1, as said below
- block_order: int32 [128], replicated, may hold values from 0 to 127, each once
Outputs:
- correlations: float32 [16, 1024, 256], P('section', 'blk')
Inputs may be any that keep to these rules, and one draw needn't show every extreme that they name: `valid_mask`: a station either has no valid segment at all, or each of its segments is valid independently. `block_order`: each block index once.
All inputs are finite; a program needn't handle non-finite values.
Results may differ from a plain program's by a relative error of at most 0.0063.
Values may be sent and summed in bfloat16 or wider, within the bound.
A program may use at most 64 MiB of HBM per device.

v0:
```python
import math
import jax
import jax.numpy as jnp
from jax import lax
from jax.sharding import PartitionSpec as P

L = 1024
NF = 384
BIN_LO = 8
LAGS = 256
TAPS = 33
HW = 50
WF = 32
STEPS = 2
RIM = 66


def extended(x, sides, width):
    for axis, dim in sides:
        devices, length = (lax.axis_size(axis), x.shape[dim])
        up = [(i, (i + 1) % devices) for i in range(devices - 1)]
        down = [(j, i) for i, j in up]
        last = lax.slice_in_dim(x, length - width, length, axis=dim)
        initial = lax.slice_in_dim(x, 0, width, axis=dim)
        before = lax.ppermute(last, axis, up)
        after = lax.ppermute(initial, axis, down)
        x = jnp.concatenate([before, x, after], axis=dim)
    return x


def from_root(value, axis, source):
    kept = jnp.where(lax.axis_index(axis) == source, value, 0).astype(value.dtype)
    return lax.psum(kept, axis)


def bandpass_taps():
    offsets = jnp.arange(TAPS, dtype=jnp.float32) - (TAPS - 1) // 2
    low = BIN_LO / L
    high = (BIN_LO + NF) / L
    window = 0.5 + 0.5 * jnp.cos(2.0 * math.pi * offsets / (TAPS + 1))
    return window * (
        2.0 * high * jnp.sinc(2.0 * high * offsets) - 2.0 * low * jnp.sinc(2.0 * low * offsets)
    )


def filter_normalize(padded):
    taps = bandpass_taps()
    width = padded.shape[1] - (TAPS - 1)
    filtered = taps[0] * padded[:, 0:width]
    for offset in range(1, TAPS):
        filtered = filtered + taps[offset] * padded[:, offset : offset + width]
    magnitude = jnp.abs(filtered)
    window_sum = lax.reduce_window(
        magnitude, jnp.zeros((), magnitude.dtype), lax.add, (1, 2 * HW + 1), (1, 1), "VALID"
    )
    centre = filtered[:, HW : HW + window_sum.shape[1]]
    return (centre / (window_sum / (2 * HW + 1) + 1e-06)).astype(jnp.bfloat16)


def forward_table():
    times = jnp.arange(L, dtype=jnp.int32)[:, None]
    bins = BIN_LO + jnp.arange(NF, dtype=jnp.int32)[None, :]
    phase = jnp.mod(times * bins, L).astype(jnp.float32) * (2.0 * math.pi / L)
    return jnp.concatenate([jnp.cos(phase), -jnp.sin(phase)], axis=1).astype(jnp.bfloat16)


def lag_table():
    bins = BIN_LO + jnp.arange(NF, dtype=jnp.int32)[:, None]
    shifts = jnp.arange(LAGS, dtype=jnp.int32)[None, :] - LAGS // 2
    phase = jnp.mod(bins * shifts, L).astype(jnp.float32) * (2.0 * math.pi / L)
    scale = 1.0 / math.sqrt(NF)
    return jnp.concatenate([jnp.cos(phase) * scale, -jnp.sin(phase) * scale], axis=0)


def whiten(normalized, maskvals):
    stations = normalized.shape[0]
    framed = normalized.reshape(-1, L)
    spectra = jnp.dot(framed, forward_table(), preferred_element_type=jnp.float32)
    spectra = spectra.reshape(stations, -1, 2 * NF)
    real_part = spectra[:, :, :NF]
    imag_part = spectra[:, :, NF:]
    amplitude = jnp.sqrt(real_part * real_part + imag_part * imag_part)
    smooth = lax.reduce_window(
        amplitude,
        jnp.zeros((), amplitude.dtype),
        lax.add,
        (1, 1, 2 * WF + 1),
        (1, 1, 1),
        ((0, 0), (0, 0), (WF, WF)),
    )
    factor = maskvals[:, :, None] / (smooth / (2 * WF + 1) + 1e-06)
    return jnp.concatenate([real_part * factor, imag_part * factor], axis=2).astype(jnp.bfloat16)


def cross_lags(sources, receivers):
    source_real = sources[:, :, :NF]
    source_imag = sources[:, :, NF:]
    recv_real = receivers[:, :, :NF]
    recv_imag = receivers[:, :, NF:]
    real_sum = jnp.einsum(
        "jsf,isf->jif", source_real, recv_real, preferred_element_type=jnp.float32
    ) + jnp.einsum("jsf,isf->jif", source_imag, recv_imag, preferred_element_type=jnp.float32)
    imag_sum = jnp.einsum(
        "jsf,isf->jif", source_real, recv_imag, preferred_element_type=jnp.float32
    ) - jnp.einsum("jsf,isf->jif", source_imag, recv_real, preferred_element_type=jnp.float32)
    stacked = jnp.concatenate([real_sum, imag_sum], axis=2)
    count_src, count_rec = (stacked.shape[0], stacked.shape[1])
    lagged = jnp.dot(
        stacked.reshape(count_src * count_rec, 2 * NF), lag_table(), precision=lax.Precision.HIGHEST
    )
    return lagged.reshape(count_src, count_rec, LAGS)


def shards(raw_traces, valid_mask, block_order):
    padded = extended(raw_traces, (("section", 1),), RIM)
    normalized = filter_normalize(padded.astype(jnp.float32))
    maskvals = valid_mask.astype(jnp.float32)
    whitened = whiten(normalized, maskvals)
    mask_wire = valid_mask.astype(jnp.bfloat16)
    stations = whitened.shape[0]
    source_parts = []
    source_masks = []
    for position in range(STEPS):
        block_spec, block_mask = (
            from_root(whitened, "blk", block_order[position]),
            from_root(mask_wire, "blk", block_order[position]),
        )
        source_parts.append(block_spec)
        source_masks.append(block_mask)
    sources = jnp.concatenate(source_parts, axis=0)
    source_mask = jnp.concatenate(source_masks, axis=0).astype(jnp.float32)
    half_count = sources.shape[0] // 2
    section_index = lax.axis_index("section")
    partial_counts = jnp.dot(source_mask, maskvals.T, precision=lax.Precision.HIGHEST)
    counts = lax.psum(partial_counts, "section")
    start = jnp.int32(0)

    def one_block(offset):
        block_spec = lax.dynamic_slice_in_dim(sources, start + offset * stations, stations, 0)
        return cross_lags(block_spec, whitened)

    lagged = lax.map(
        one_block, jnp.arange(half_count * lax.axis_size("section") // stations, dtype=jnp.int32)
    )
    summed_lags = lax.psum_scatter(
        lagged.reshape(half_count * lax.axis_size("section"), stations, LAGS),
        "section",
        scatter_dimension=0,
        tiled=True,
    )
    own_counts = lax.dynamic_slice_in_dim(counts, section_index * half_count, half_count, 0)
    return summed_lags / jnp.maximum(own_counts, 1.0)[:, :, None]


def solution(mesh):
    return jax.shard_map(
        shards,
        mesh=mesh,
        in_specs=(P("blk", "section"), P("blk", "section"), P()),
        out_specs=P("section", "blk", None),
        check_vma=False,
    )
```

profile of v0, /device:TPU:1, one launch (start us, length us, event | category | flops | bytes accessed | tf_op | source)
XLA Modules:
  0.0 1282.6 jit_solution(17670595992251923281)
XLA Ops:
  6.5 0.8 fusion.72
  7.4 3.9 collective-permute-start
  11.3 1.3 collective-permute-start.1
  12.7 0.7 fusion.74
  13.4 6.5 cosine_convert_fusion
  22.4 0.7 fusion.75
  23.2 21.8 %fusion.69 = (f32[8,4196]{1,0:T(8,128)S(1)}, f32[8,4196]{1,0:T(8,128)S(1)}) fusion(f32[8,4228]{1,0:T(8,128)S(1)} %convert_element_type.37, f32[]{:T(128)} %bitcast.38, f32[]{:T(128)} %bitcast.37, f32[]{:T(128)} %bitcast.36, f32[]{:T(128)} %bitcast.35, f32[]{:T(128)} %bitcast.34, f32[]{:T(128)} %bitcast.33, f32[]{:T(128)} %bitcast.32, f32[]{:T(128)} %bitcast.31, ...), kind=kLoop, calls=%fused_computation.155 | loop fusion | flops 2215488 | bytes 4699652 | tf_op jit(solution)/shard_map/abs | solution.py:52
  45.0 65.2 %reduce_window.14 = f32[8,4096]{1,0:T(8,128)S(1)} reduce-window(f32[8,4196]{1,0:T(8,128)S(1)} %get-tuple-element.93, f32[]{:T(128)} %constant.132.clone.1), window={size=1x101}, to_apply=%region_0.2 | reduce-window | flops 3276800 | bytes 265348 | tf_op jit(solution)/shard_map/reduce_window | solution.py:53
  110.7 12.9 %reduce_window.15 = f32[8,4,384]{2,0,1:T(8,128)S(1)} reduce-window(f32[8,4,384]{2,0,1:T(8,128)S(1)} %add_sqrt_fusion, f32[]{:T(128)} %constant.132.clone.1), window={size=1x1x65 pad=0_0x0_0x32_32}, to_apply=%region_1.3 | reduce-window | flops 786432 | bytes 98308 | tf_op jit(solution)/shard_map/reduce_window | solution.py:83
  124.5 1116.5 %all-reduce.3.cloned.1.call-done = (bf16[8,4,768]{2,0,1:T(8,128)(2,1)}, bf16[8,4,768]{2,0,1:T(8,128)(2,1)}, bf16[8,4]{0,1:T(4,128)(2,1)}, bf16[8,4]{0,1:T(4,128)(2,1)}) async-done(((bf16[8,4,768]{2,0,1:T(8,128)(2,1)}, bf16[8,4,768]{2,0,1:T(8,128)(2,1)}, bf16[8,4]{0,1:T(4,128)(2,1)}, bf16[8,4]{0,1:T(4,128)(2,1)}), (bf16[8,4,768]{2,0,1:T(8,128)(2,1)}, bf16[8,4,768]{2,0,1:T(8,128)(2,1)}, ...) | async-done | bytes 98448 | tf_op jit(solution)/shard_map/psum | solution.py:33
  1241.0 0.8 pad_maximum_fusion
  1241.9 19.7 %while.12 = (s32[]{:T(128)}, f32[2,8,8,256]{3,2,1,0:T(8,128)}, s32[2]{0:T(128)S(1)}, bf16[16,4,768]{2,0,1:T(8,128)(2,1)S(1)}, bf16[8,4,768]{2,1,0:T(4,128)(2,1)S...) while((s32[]{:T(128)}, f32[2,8,8,256]{3,2,1,0:T(8,128)}, s32[2]{0:T(128)S(1)}, ...), condition=%wide.region_5.7_spmd, body=%wide.region_4.6_spmd.sunk | while | flops 153748096 | bytes 4200115 | solution.py:142
  1243.7 0.6 fusion.114
  1246.5 0.7 fusion.116
  1247.7 0.7 fusion.117
  1249.0 1.6 cosine_multiply_fusion.2
  1250.6 1.1 fusion.118
  1256.4 0.7 fusion.116
  1257.6 0.7 fusion.117
  1258.8 1.6 cosine_multiply_fusion.2
  1260.4 1.2 fusion.118
  1261.9 3.8 psum.39
  1265.7 8.3 reduce-scatter.2.cloned.1.call-done
  1274.0 1.5 broadcast_divide_fusion
  (64 shorter events, 12.3 us)
Async XLA Ops:
  6.5 16.6 %copy-start = (bf16[8,4096]{1,0:T(8,128)(2,1)S(1)}, bf16[8,4096]{1,0:T(8,128)(2,1)}, u32[]{:S(2)}) copy-start(bf16[8,4096]{1,0:T(8,128)(2,1)} %param.6) | copy-start | bytes 196612
  6.5 13.4 %copy-start.2 = (s32[128]{0:T(128)S(1)}, s32[128]{0:T(128)}, u32[]{:S(2)}) copy-start(s32[128]{0:T(128)} %param.8) | copy-start | bytes 1540
  6.5 15.2 %copy-start.1 = (s32[8,4]{0,1:T(4,128)S(1)}, s32[8,4]{0,1:T(4,128)}, u32[]{:S(2)}) copy-start(s32[8,4]{0,1:T(4,128)} %param.7) | copy-start | bytes 388
  6.5 1234.5 %all-reduce.3.cloned.1.call-start = ((), (), s32[]{:S(2)}) async-start(), calls=%async_computation.2 | async-start | bytes 200704 | tf_op jit(solution)/shard_map/psum | solution.py:33
  7.4 15.7 %collective-permute-start = (bf16[8,66]{1,0:T(8,128)(2,1)S(1)}, bf16[8,66]{1,0:T(8,128)(2,1)S(1)}, u32[]{:S(2)}, u32[]{:S(2)}) collective-permute-start(bf16[8,66]{1,0:T(8,128)(2,1)S(1)} %get-tuple-element.106), channel_id=1, source_target_pairs={{0,128},{1,129},{2,130},{3,131},{4,132},{5,133},{6,134},{7,135},{8... | collective-permute-start | bytes 3176 | tf_op jit(solution)/shard_map/ppermute | solution.py:25
  11.3 11.8 collective-permute-start.1
  124.4 1149.7 %reduce-scatter.2.cloned.1.call-start = ((), (), s32[]{:S(2)}) async-start(), calls=%async_computation.1 | async-start | bytes 196608 | tf_op jit(solution)/shard_map/reduce_scatter | solution.py:145
  1241.8 19.8 %copy-start.3 = (bf16[8,4]{0,1:T(4,128)(2,1)S(1)}, bf16[8,4]{0,1:T(4,128)(2,1)}, u32[]{:S(2)}) copy-start(bf16[8,4]{0,1:T(4,128)(2,1)} %get-tuple-element.91) | copy-start | bytes 196
  1241.8 19.8 %copy-start.4 = (bf16[8,4]{0,1:T(4,128)(2,1)S(1)}, bf16[8,4]{0,1:T(4,128)(2,1)}, u32[]{:S(2)}) copy-start(bf16[8,4]{0,1:T(4,128)(2,1)} %get-tuple-element.92) | copy-start | bytes 196
Sparse Core Ops, SparseCore 0:
  124.5 1116.4 all-reduce.2
  1261.7 12.2 reduce-scatter.1
where the time goes:
time: 1290 us; the launch traced here: 1280 us
  waiting for transfers between devices  1120 us (87%)
  other arithmetic  114 us (9%)
  between operations  15.1 us (1%)
    psum x1, waiting for transfers between devices, from_root(): return lax.psum(kept, axis)  1120 us
    another operation x1, other arithmetic, filter_normalize(): lax.reduce_window(magnitude, jnp.zeros((), magnitude.dtype), lax.add, (1,...  65.2 us
  transfers between devices with their start and end apart: 4, of which 2 were waited for; matrix products, arithmetic and copies ran while one was open for 1% of the time, Pallas kernels for 0%

commit v1 on v0

--- a/solution.py
+++ b/solution.py
@@ -15,6 +15,10 @@
 RIM = 66
 
 
+def recover_records(panel, shard_axis):
+    return jnp.sum(lax.all_gather(panel, shard_axis), 0)
+
+
 def extended(x, sides, width):
     for axis, dim in sides:
         devices, length = (lax.axis_size(axis), x.shape[dim])
@@ -30,7 +34,7 @@
 
 def from_root(value, axis, source):
     kept = jnp.where(lax.axis_index(axis) == source, value, 0).astype(value.dtype)
-    return lax.psum(kept, axis)
+    return recover_records(kept, axis)
 
 
 def bandpass_taps():

time: 1290 us -> 534 us (0.41)
  waiting for transfers between devices: 1120 us -> 5.77 us
  blocking collectives: 3.83 us -> 366 us
    psum x1 -> x0, waiting for transfers between devices: 1120 us -> none  [from_root(): return lax.psum(kept, axis)]
    all_gather x0 -> x2, blocking collectives: none -> 362 us  [recover_records(): return jnp.sum(lax.all_gather(panel, shard_axis), 0)]
  transfers between devices with their start and end apart: 4 -> 5, of which waited for: 2 -> 1; matrix products, arithmetic and copies ran while one was open for 1% -> 2% of each run, Pallas kernels for 0% -> 0%
where the time goes in v1:
time: 534 us; the launch traced here: 523 us
  blocking collectives  366 us (69%)
  other arithmetic  111 us (21%)
  between operations  15 us (3%)
  local copies, waits for them, and re-layouts  11.6 us (2%)
  matrix products  6.89 us (1%)
  waiting for transfers between devices  5.77 us (1%)
    all_gather x2, blocking collectives, recover_records(): return jnp.sum(lax.all_gather(panel, shard_axis), 0)  362 us
    another operation x1, other arithmetic, filter_normalize(): lax.reduce_window(magnitude, jnp.zeros((), magnitude.dtype), lax.add, (1,...  56.6 us
    abs x1, other arithmetic, filter_normalize(): magnitude = jnp.abs(filtered)  21.9 us
    another operation x1, other arithmetic, whiten(): lax.reduce_window(amplitude, jnp.zeros((), amplitude.dtype), lax.add, (1,...  12.9 us
  transfers between devices with their start and end apart: 5, of which 1 were waited for; matrix products, arithmetic and copies ran while one was open for 2% of the time, Pallas kernels for 0%

profile of v1, /device:TPU:1, one launch (start us, length us, event | category | flops | bytes accessed | tf_op | source)
XLA Modules:
  0.0 523.4 jit_solution(5941018040268232980)
XLA Ops:
  6.5 0.8 fusion.72
  7.4 3.9 collective-permute-start
  11.3 1.3 collective-permute-start.1
  12.7 0.7 fusion.74
  13.4 0.7 fusion.75
  14.1 6.5 %cosine_convert_fusion = (bf16[1024,384]{1,0:T(8,128)(2,1)S(1)}, bf16[1024,384]{1,0:T(8,128)(2,1)S(1)}) fusion(s32[384]{0:T(512)S(1)} %iota_add_fusion.2), kind=kLoop, calls=%fused_computation.33 | loop fusion | flops 6684672 | bytes 1574400 | tf_op jit(solution)/shard_map/convert.10
  22.6 21.9 %fusion.69 = (f32[8,4196]{1,0:T(8,128)S(1)}, f32[8,4196]{1,0:T(8,128)S(1)}) fusion(f32[8,4228]{1,0:T(8,128)S(1)} %convert_element_type.56, f32[]{:T(128)} %bitcast.38, f32[]{:T(128)} %bitcast.37, f32[]{:T(128)} %bitcast.36, f32[]{:T(128)} %bitcast.35, f32[]{:T(128)} %bitcast.34, f32[]{:T(128)} %bitcast.33, f32[]{:T(128)} %bitcast.32, f32[]{:T(128)} %bitcast.31, ...), kind=kLoop, calls=%fused_computation.156 | loop fusion | flops 2215488 | bytes 4699652 | tf_op jit(solution)/shard_map/abs | solution.py:56
  44.5 56.6 %reduce_window.14 = f32[8,4096]{1,0:T(8,128)S(1)} reduce-window(f32[8,4196]{1,0:T(8,128)S(1)} %get-tuple-element.94, f32[]{:T(128)} %constant.136.clone.1), window={size=1x101}, to_apply=%region_0.2 | reduce-window | flops 3276800 | bytes 265348 | tf_op jit(solution)/shard_map/reduce_window | solution.py:57
  101.6 12.9 %reduce_window.15 = f32[8,4,384]{2,0,1:T(8,128)S(1)} reduce-window(f32[8,4,384]{2,0,1:T(8,128)S(1)} %add_sqrt_fusion, f32[]{:T(128)} %constant.136.clone.1), window={size=1x1x65 pad=0_0x0_0x32_32}, to_apply=%region_1.3 | reduce-window | flops 786432 | bytes 98308 | tf_op jit(solution)/shard_map/reduce_window | solution.py:87
  115.3 0.7 all-gather.9.cloned.1.call-update
  116.1 186.2 %all-gather.2 = bf16[128,8,4]{1,2,0:T(4,128)(2,1)S(1)} all-gather(bf16[1,8,4]{1,2,0:T(4,128)(2,1)S(1)} %get-tuple-element.110), channel_id=2, replica_groups=mesh['section'=2,'blk'=128] {'blk'}, dimensions={0}, use_global_device_ids=true | all-gather | bytes 8256 | tf_op jit(solution)/shard_map/all_gather | solution.py:19
  302.4 175.3 %all-gather.3 = bf16[128,8,4]{1,2,0:T(4,128)(2,1)S(1)} all-gather(bf16[1,8,4]{1,2,0:T(4,128)(2,1)S(1)} %get-tuple-element.111), channel_id=3, replica_groups=mesh['section'=2,'blk'=128] {'blk'}, dimensions={0}, use_global_device_ids=true | all-gather | bytes 8256 | tf_op jit(solution)/shard_map/all_gather | solution.py:19
  478.0 3.7 reduce_sum.48
  481.7 3.7 reduce_sum.49
  485.4 20.1 %while.12 = (s32[]{:T(128)}, f32[2,8,8,256]{3,2,1,0:T(8,128)}, s32[2]{0:T(128)S(1)}, bf16[16,4,768]{2,0,1:T(8,128)(2,1)S(1)}, bf16[8,4,768]{2,1,0:T(4,128)(2,1)S...) while((s32[]{:T(128)}, f32[2,8,8,256]{3,2,1,0:T(8,128)}, s32[2]{0:T(128)S(1)}, ...), condition=%wide.region_5.7_spmd, body=%wide.region_4.6_spmd.sunk | while | flops 153748096 | bytes 5248239 | solution.py:146
  490.4 0.7 fusion.116
  491.5 0.7 fusion.117
  492.8 1.6 cosine_multiply_fusion.2
  500.3 0.7 fusion.116
  501.4 0.7 fusion.117
  502.7 1.6 cosine_multiply_fusion.2
  505.8 4.1 psum.7
  509.9 5.0 reduce-scatter.2.cloned.1.call-done
  514.9 1.5 broadcast_divide_fusion
  (78 shorter events, 15.1 us)
Async XLA Ops:
  6.5 16.0 %copy-start.2 = (bf16[8,4096]{1,0:T(8,128)(2,1)S(1)}, bf16[8,4096]{1,0:T(8,128)(2,1)}, u32[]{:S(2)}) copy-start(bf16[8,4096]{1,0:T(8,128)(2,1)} %param.6) | copy-start | bytes 196612
  6.5 14.1 %copy-start.4 = (s32[128]{0:T(128)S(1)}, s32[128]{0:T(128)}, u32[]{:S(2)}) copy-start(s32[128]{0:T(128)} %param.8) | copy-start | bytes 1540
  6.5 14.7 %copy-start.3 = (s32[8,4]{0,1:T(4,128)S(1)}, s32[8,4]{0,1:T(4,128)}, u32[]{:S(2)}) copy-start(s32[8,4]{0,1:T(4,128)} %param.7) | copy-start | bytes 388
  6.5 471.4 %all-gather.7.cloned.1.call-start = ((), (), s32[]{:S(2)}) async-start(), calls=%async_computation.1 | async-start | bytes 6340608 | tf_op jit(solution)/shard_map/all_gather | solution.py:19
  7.4 15.1 %collective-permute-start = (bf16[8,66]{1,0:T(8,128)(2,1)S(1)}, bf16[8,66]{1,0:T(8,128)(2,1)S(1)}, u32[]{:S(2)}, u32[]{:S(2)}) collective-permute-start(bf16[8,66]{1,0:T(8,128)(2,1)S(1)} %get-tuple-element.107), channel_id=1, source_target_pairs={{0,128},{1,129},{2,130},{3,131},{4,132},{5,133},{6,134},{7,135},{8... | collective-permute-start | bytes 3176 | tf_op jit(solution)/shard_map/ppermute | solution.py:29
  11.3 11.2 %collective-permute-start.1 = (bf16[8,66]{1,0:T(8,128)(2,1)S(1)}, bf16[8,66]{1,0:T(8,128)(2,1)S(1)}, u32[]{:S(2)}, u32[]{:S(2)}) collective-permute-start(bf16[8,66]{1,0:T(8,128)(2,1)S(1)} %get-tuple-element.106), channel_id=1, source_target_pairs={{128,0},{129,1},{130,2},{131,3},{132,4},{133,5},{134,6},{135,7},{1... | collective-permute-start | bytes 3176 | tf_op jit(solution)/shard_map/ppermute | solution.py:30
  115.2 366.5 %all-gather.9.cloned.1.call-start = ((), (), s32[]{:S(2)}) async-start(), calls=%async_computation.2 | async-start | bytes 6340608 | tf_op jit(solution)/shard_map/all_gather | solution.py:19
  116.0 398.9 %reduce-scatter.2.cloned.1.call-start = ((), (), s32[]{:S(2)}) async-start(), calls=%async_computation.3 | async-start | bytes 196608 | tf_op jit(solution)/shard_map/reduce_scatter | solution.py:149
  492.2 2.2 copy-start
  494.9 0.7 copy-start.1
  502.1 2.2 copy-start
  504.9 0.7 copy-start.1
Sparse Core Ops, SparseCore 0:
  115.3 128.8 all-gather.6
  248.0 120.7 all-gather.8
  505.6 9.2 reduce-scatter.1
